TPU v7x, 32 devices: a whole 2x2x4 slice. The times are simulated.
32 devices in a mesh: rep: 4 (over y, x), seq: 8 (over z, core).
Axes of the slice: x: 2, y: 2, z: 4, core: 2. Of those that a mesh axis runs over, the one named last changes fastest.
Arguments:
- inputs: bfloat16 [4, 2048, 1536], P('rep', 'seq'), may hold values from -13 to 13
- segment_ids: int32 [4, 2048], P('rep'), may hold values from 0 to 7, as said below
- valid_mask: int32 [4, 2048], P('rep'), may hold values from 0 to 1, as said below
- input_weight: bfloat16 [1536, 4608], P('seq'), may hold values from -0.15625 to 0.15625
- output_weight: bfloat16 [1536, 1536], P('seq'), may hold values from -0.15625 to 0.15625
- conv_kernel: float32 [16, 6, 11], replicated, may hold values from -1.2 to 1.2
- head_mix: float32 [8, 2, 2], replicated, may hold values from 0.2 to 1
- first_gain: float32 [1536], replicated, may hold values from 0.5 to 1.5
- second_gain: float32 [1536], replicated, may hold values from 0.5 to 1.5
- group_gain: float32 [1536], replicated, may hold values from 0.5 to 1.5
- gate_weight: bfloat16 [1536, 4096], P(None, 'seq'), may hold values from -0.15625 to 0.15625
- up_weight: bfloat16 [1536, 4096], P(None, 'seq'), may hold values from -0.15625 to 0.15625
- down_weight: bfloat16 [4096, 1536], P('seq'), may hold values from -0.09375 to 0.09375
- cotangent: bfloat16 [4, 2048, 1536], P('rep', 'seq'), may hold values from -17 to 17
Outputs:
- output: bfloat16 [4, 2048, 1536], P('rep', 'seq')
- grad_inputs: bfloat16 [4, 2048, 1536], P('rep', 'seq')
- grad_input_weight: float32 [1536, 4608], P('seq')
- grad_output_weight: float32 [1536, 1536], P('seq')
- grad_kernel: float32 [16, 6, 11], replicated
- grad_mix: float32 [8, 2, 2], replicated
- grad_first_gain: float32 [1536], replicated
- grad_second_gain: float32 [1536], replicated
- grad_group_gain: float32 [1536], replicated
- grad_gate: float32 [1536, 4096], P(None, 'seq')
- grad_up: float32 [1536, 4096], P(None, 'seq')
- grad_down: float32 [4096, 1536], P('seq')
Inputs may be any that keep to these rules, and one draw needn't show every extreme that they name: `segment_ids`: segment ids never fall along a sequence and start at 0. The positions k * 1024 to (k + 1) * 1024 - 1 form frame k; every document lies inside one frame, a frame holds one to four documents, the first frame of the first sequence is a single document of exactly 1024 positions, and every frame of the last sequence holds four documents. `valid_mask`: in each frame the positions with 0 form its tail, at most 256 of them; the first frame of the first sequence has none.
All inputs are finite; a program needn't handle non-finite values.
Results may differ from a plain program's by a relative error of at most 0.02.
Values may be sent and summed in bfloat16 or wider, within the bound.
A program may use at most 384 MiB of HBM per device.

v0:
```python
import jax
import jax.numpy as jnp
from jax import lax
from jax.sharding import PartitionSpec as P

REACH = 4
EPS = 1e-06
HIGHEST = lax.Precision.HIGHEST


def from_behind(x, axis, by):
    count = lax.axis_size(axis)
    pairs = [(i, i + by) for i in range(count) if 0 <= i + by < count]
    return lax.ppermute(x, axis, pairs)


def convolve(logits, kernel, rows, columns):
    rim_rows = kernel.shape[1] - 1
    key_span = kernel.shape[2] - 1
    result = jnp.zeros((logits.shape[0], rows, columns), jnp.float32)
    for row_tap in range(kernel.shape[1]):
        for col_tap in range(kernel.shape[2]):
            weight = kernel[:, row_tap, col_tap][:, None, None]
            result = (
                result
                + weight
                * logits[
                    :,
                    rim_rows - row_tap : rim_rows - row_tap + rows,
                    key_span - col_tap : key_span - col_tap + columns,
                ]
            )
    return result


def convolve_back(grads, kernel):
    rim_rows = kernel.shape[1] - 1
    key_span = kernel.shape[2] - 1
    rows = grads.shape[1] + rim_rows
    columns = grads.shape[2] + key_span
    padded = jnp.pad(grads, ((0, 0), (rim_rows, rim_rows), (key_span, key_span)))
    result = jnp.zeros((grads.shape[0], rows, columns), jnp.float32)
    for row_tap in range(kernel.shape[1]):
        for col_tap in range(kernel.shape[2]):
            weight = kernel[:, row_tap, col_tap][:, None, None]
            result = (
                result + weight * padded[:, row_tap : row_tap + rows, col_tap : col_tap + columns]
            )
    return result


def kernel_grads(grads, logits, taps_rows, taps_cols):
    rim_rows = taps_rows - 1
    key_span = taps_cols - 1
    rows = grads.shape[1]
    columns = grads.shape[2]
    entries = []
    for row_tap in range(taps_rows):
        line_sums = []
        for col_tap in range(taps_cols):
            window_part = logits[
                :,
                rim_rows - row_tap : rim_rows - row_tap + rows,
                key_span - col_tap : key_span - col_tap + columns,
            ]
            line_sums.append(jnp.sum(grads * window_part, axis=(1, 2)))
        entries.append(jnp.stack(line_sums, axis=-1))
    return jnp.stack(entries, axis=1)


def attend_group(operands, mask_ext, mask_own, row_valid, score_scale):
    query_g, key_g, value_g, kernel_g, mixing_g = operands
    rows = mask_own.shape[0]
    columns = mask_own.shape[1]
    raw = jnp.einsum("qhd,khd->hqk", query_g, key_g, preferred_element_type=jnp.float32)
    logits = raw * score_scale * mask_ext
    conv = convolve(logits, kernel_g, rows, columns)
    allowed = mask_own > 0
    peak = jnp.max(jnp.where(allowed, conv, -1e30), axis=-1, keepdims=True)
    peak = jnp.where(row_valid > 0, peak, 0.0)
    expo = jnp.where(allowed, jnp.exp(conv - peak), 0.0)
    denom = jnp.sum(expo, axis=-1, keepdims=True) + 1.0 - row_valid
    prob = expo / denom
    mixed = (
        mixing_g[:, 0][:, None, None] * prob[0][None]
        + mixing_g[:, 1][:, None, None] * prob[1][None]
    )
    mixed_low = mixed.astype(jnp.bfloat16)
    result = jnp.einsum("hqk,khd->qhd", mixed_low, value_g, preferred_element_type=jnp.float32)
    return (result, peak + jnp.log(denom))


def attend_group_back(operands, mask_ext, mask_own, score_scale):
    query_g, key_g, value_g, kernel_g, mixing_g, dresult_g, lse_g = operands
    rows = mask_own.shape[0]
    columns = mask_own.shape[1]
    raw = jnp.einsum("qhd,khd->hqk", query_g, key_g, preferred_element_type=jnp.float32)
    logits = raw * score_scale * mask_ext
    conv = convolve(logits, kernel_g, rows, columns)
    allowed = mask_own > 0
    prob = jnp.where(allowed, jnp.exp(conv - lse_g), 0.0)
    mixed = (
        mixing_g[:, 0][:, None, None] * prob[0][None]
        + mixing_g[:, 1][:, None, None] * prob[1][None]
    )
    mixed_low = mixed.astype(jnp.bfloat16)
    dmixed = jnp.einsum("qhd,khd->hqk", dresult_g, value_g, preferred_element_type=jnp.float32)
    dvalue = jnp.einsum("hqk,qhd->khd", mixed_low, dresult_g, preferred_element_type=jnp.float32)
    dmixing = jnp.stack(
        [
            jnp.sum(dmixed * prob[0][None], axis=(1, 2)),
            jnp.sum(dmixed * prob[1][None], axis=(1, 2)),
        ],
        axis=-1,
    )
    dprob = (
        mixing_g[0][:, None, None] * dmixed[0][None] + mixing_g[1][:, None, None] * dmixed[1][None]
    )
    dconv = prob * (dprob - jnp.sum(prob * dprob, axis=-1, keepdims=True))
    dkernel = kernel_grads(dconv, logits, kernel_g.shape[1], kernel_g.shape[2])
    dlogits = convolve_back(dconv, kernel_g) * mask_ext * score_scale
    dquery = jnp.einsum(
        "hqk,khd->qhd",
        dlogits,
        key_g.astype(jnp.float32),
        precision=HIGHEST,
        preferred_element_type=jnp.float32,
    )
    dkey = jnp.einsum(
        "hqk,qhd->khd",
        dlogits,
        query_g.astype(jnp.float32),
        precision=HIGHEST,
        preferred_element_type=jnp.float32,
    )
    return (dquery, dkey, dvalue, dkernel, dmixing)


def rms_scale(values):
    return lax.rsqrt(jnp.mean(values * values, axis=-1, keepdims=True) + EPS)


def norm_back(grad_out, values, inv_scale, gain):
    scaled_grad = grad_out * gain
    inner = jnp.mean(scaled_grad * values, axis=-1, keepdims=True)
    return inv_scale * scaled_grad - values * inv_scale**3 * inner


def on_device(
    inputs,
    segment_ids,
    valid_mask,
    input_weight,
    output_weight,
    conv_kernel,
    head_mix,
    first_gain,
    second_gain,
    group_gain,
    gate_weight,
    up_weight,
    down_weight,
    cotangent,
):
    tokens = inputs.shape[1]
    model_width = inputs.shape[2]
    head_count = conv_kernel.shape[0]
    head_dim = model_width // head_count
    groups = head_mix.shape[0]
    rim_rows = conv_kernel.shape[1] - 1
    half_span = conv_kernel.shape[2] // 2
    window = REACH * tokens
    score_scale = head_dim ** (-0.5)
    seq_rank = lax.axis_index("seq")
    row_start = seq_rank * tokens
    window_start = row_start - (REACH - 1) * tokens
    resid_in = inputs[0].astype(jnp.float32)
    grad_out = cotangent[0].astype(jnp.float32)
    offset = window + half_span
    segment_pad = jnp.concatenate(
        [jnp.full((offset,), -1, jnp.int32), segment_ids[0], jnp.full((half_span,), -1, jnp.int32)]
    )
    valid_pad = jnp.concatenate(
        [jnp.zeros((offset,), jnp.int32), valid_mask[0], jnp.zeros((half_span,), jnp.int32)]
    )
    query_pos = row_start - rim_rows + jnp.arange(tokens + rim_rows, dtype=jnp.int32)
    key_pos = window_start - half_span + jnp.arange(window + 2 * half_span, dtype=jnp.int32)
    query_seg = lax.dynamic_slice_in_dim(
        segment_pad, row_start - rim_rows + offset, tokens + rim_rows
    )
    key_seg = lax.dynamic_slice_in_dim(
        segment_pad, window_start - half_span + offset, window + 2 * half_span
    )
    query_live = lax.dynamic_slice_in_dim(
        valid_pad, row_start - rim_rows + offset, tokens + rim_rows
    )
    key_live = lax.dynamic_slice_in_dim(
        valid_pad, window_start - half_span + offset, window + 2 * half_span
    )
    mask_ext = (
        (query_seg[:, None] == key_seg[None, :])
        & (key_pos[None, :] <= query_pos[:, None])
        & (query_live[:, None] > 0)
        & (key_live[None, :] > 0)
    ).astype(jnp.float32)
    mask_own = mask_ext[rim_rows:, half_span : half_span + window]
    row_valid = query_live[rim_rows:].astype(jnp.float32)[:, None]
    full_input, full_output = (
        lax.all_gather(input_weight, "seq", axis=0, tiled=True),
        lax.all_gather(output_weight, "seq", axis=0, tiled=True),
    )
    first_scale = rms_scale(resid_in)
    normed_in = (resid_in * first_scale * first_gain).astype(jnp.bfloat16)
    projected = jnp.dot(normed_in, full_input, preferred_element_type=jnp.float32).astype(
        jnp.bfloat16
    )
    query = projected[:, :model_width]
    keys_values = projected[:, model_width:]
    query_rim = from_behind(query[tokens - rim_rows :], "seq", 1)
    query_ext = jnp.concatenate([query_rim, query], axis=0)
    pieces = [keys_values]
    for distance in range(1, REACH):
        pieces.append(from_behind(keys_values, "seq", distance))
    window_rows = jnp.concatenate(pieces[::-1], axis=0)
    key_ext = jnp.pad(window_rows[:, :model_width], ((half_span, half_span), (0, 0)))
    value_window = window_rows[:, model_width:]

    def split_heads(values):
        return values.reshape(values.shape[0], groups, 2, head_dim).transpose(1, 0, 2, 3)

    def merge_heads(values):
        return values.transpose(1, 0, 2, 3).reshape(values.shape[1], model_width)

    query_groups = split_heads(query_ext)
    key_groups = split_heads(key_ext)
    value_groups = split_heads(value_window)
    kernel_groups = conv_kernel.reshape(groups, 2, conv_kernel.shape[1], conv_kernel.shape[2])
    result_groups, lse_groups = lax.map(
        lambda operands: attend_group(operands, mask_ext, mask_own, row_valid, score_scale),
        (query_groups, key_groups, value_groups, kernel_groups, head_mix),
    )
    attended = merge_heads(result_groups)
    shaped = attended.reshape(tokens, head_count, head_dim)
    centred = shaped - jnp.mean(shaped, axis=-1, keepdims=True)
    inv_std = lax.rsqrt(jnp.mean(centred * centred, axis=-1, keepdims=True) + EPS)
    unit_heads = centred * inv_std
    unit = unit_heads.reshape(tokens, model_width)
    normed = (unit * group_gain).astype(jnp.bfloat16)
    branch = jnp.dot(normed, full_output, preferred_element_type=jnp.float32)
    resid = resid_in + row_valid * branch
    second_scale = rms_scale(resid)
    normed_mid = (resid * second_scale * second_gain).astype(jnp.bfloat16)
    dmlp = (row_valid * grad_out).astype(jnp.bfloat16)
    contract_rows = (((0,), (0,)), ((), ()))
    inputs_all = lax.all_gather(normed_mid, "seq", axis=0, tiled=True)
    gate = jnp.dot(inputs_all, gate_weight, preferred_element_type=jnp.float32)
    up_proj = jnp.dot(inputs_all, up_weight, preferred_element_type=jnp.float32)
    hidden = (jax.nn.silu(gate) * up_proj).astype(jnp.bfloat16)
    mlp = lax.psum_scatter(
        jnp.dot(hidden, down_weight, preferred_element_type=jnp.float32).astype(jnp.bfloat16),
        "seq",
        scatter_dimension=0,
        tiled=True,
    ).astype(jnp.float32)
    result = resid + row_valid * mlp
    dmlp_all = lax.all_gather(dmlp, "seq", axis=0, tiled=True)
    dhidden = jnp.dot(dmlp_all, down_weight.T, preferred_element_type=jnp.float32)
    sigmoid_gate = jax.nn.sigmoid(gate)
    gate_grad = (dhidden * up_proj * sigmoid_gate * (1.0 + gate * (1.0 - sigmoid_gate))).astype(
        jnp.bfloat16
    )
    up_grad = (dhidden * gate * sigmoid_gate).astype(jnp.bfloat16)
    grad_down = lax.dot_general(hidden, dmlp_all, contract_rows, preferred_element_type=jnp.float32)
    grad_gate = lax.dot_general(
        inputs_all, gate_grad, contract_rows, preferred_element_type=jnp.float32
    )
    grad_up = lax.dot_general(
        inputs_all, up_grad, contract_rows, preferred_element_type=jnp.float32
    )
    dmid = lax.psum_scatter(
        (
            jnp.dot(gate_grad, gate_weight.T, preferred_element_type=jnp.float32)
            + jnp.dot(up_grad, up_weight.T, preferred_element_type=jnp.float32)
        ).astype(jnp.bfloat16),
        "seq",
        scatter_dimension=0,
        tiled=True,
    ).astype(jnp.float32)
    second_part = jnp.sum(dmid * resid * second_scale, axis=0)
    dresid = grad_out + norm_back(dmid, resid, second_scale, second_gain)
    dbranch = (row_valid * dresid).astype(jnp.bfloat16)
    whole_output_grad = lax.dot_general(
        normed, dbranch, contract_rows, preferred_element_type=jnp.float32
    )
    dnormed = jnp.dot(dbranch, full_output.T, preferred_element_type=jnp.float32)
    group_part = jnp.sum(dnormed * unit, axis=0)
    dunit = (dnormed * group_gain).reshape(tokens, head_count, head_dim)
    dshaped = inv_std * (
        dunit
        - jnp.mean(dunit, axis=-1, keepdims=True)
        - unit_heads * jnp.mean(dunit * unit_heads, axis=-1, keepdims=True)
    )
    dattended = dshaped.reshape(tokens, model_width).astype(jnp.bfloat16)
    dquery_g, dkey_g, dvalue_g, dkernel_g, dmixing = lax.map(
        lambda operands: attend_group_back(operands, mask_ext, mask_own, score_scale),
        (
            query_groups,
            key_groups,
            value_groups,
            kernel_groups,
            head_mix,
            split_heads(dattended),
            lse_groups,
        ),
    )
    dquery_ext = merge_heads(dquery_g)
    dkey_window = merge_heads(dkey_g)[half_span : half_span + window]
    dvalue_window = merge_heads(dvalue_g)
    dpair_window = jnp.concatenate([dkey_window, dvalue_window], axis=1)
    dpair = dpair_window[(REACH - 1) * tokens :]
    for distance in range(1, REACH):
        block_first = (REACH - 1 - distance) * tokens
        dpair = dpair + from_behind(
            dpair_window[block_first : block_first + tokens].astype(jnp.bfloat16), "seq", -distance
        ).astype(jnp.float32)
    rim_grad = from_behind(dquery_ext[:rim_rows], "seq", -1)
    dquery_own = dquery_ext[rim_rows:]
    dquery_own = jnp.concatenate(
        [dquery_own[: tokens - rim_rows], dquery_own[tokens - rim_rows :] + rim_grad], axis=0
    )
    dprojected = jnp.concatenate([dquery_own, dpair], axis=1).astype(jnp.bfloat16)
    whole_input_grad = lax.dot_general(
        normed_in, dprojected, contract_rows, preferred_element_type=jnp.float32
    )
    dnormin = jnp.dot(dprojected, full_input.T, preferred_element_type=jnp.float32)
    first_part = jnp.sum(dnormin * resid_in * first_scale, axis=0)
    grad_in = dresid + norm_back(dnormin, resid_in, first_scale, first_gain)
    input_shard, output_shard = (
        lax.psum_scatter(
            whole_input_grad.astype(jnp.bfloat16), "seq", scatter_dimension=0, tiled=True
        ).astype(jnp.float32),
        lax.psum_scatter(
            whole_output_grad.astype(jnp.bfloat16), "seq", scatter_dimension=0, tiled=True
        ).astype(jnp.float32),
    )
    kernel_part = dkernel_g.reshape(head_count, conv_kernel.shape[1], conv_kernel.shape[2])
    grad_kernel, grad_mix, grad_first, grad_second, grad_group = lax.psum(
        (kernel_part, dmixing, first_part, second_part, group_part), ("rep", "seq")
    )
    grad_input_w, grad_output_w, grad_gate, grad_up, grad_down = (
        lax.psum(input_shard.astype(jnp.bfloat16), "rep").astype(jnp.float32),
        lax.psum(output_shard.astype(jnp.bfloat16), "rep").astype(jnp.float32),
        lax.psum(grad_gate.astype(jnp.bfloat16), "rep").astype(jnp.float32),
        lax.psum(grad_up.astype(jnp.bfloat16), "rep").astype(jnp.float32),
        lax.psum(grad_down.astype(jnp.bfloat16), "rep").astype(jnp.float32),
    )
    return (
        result.astype(jnp.bfloat16)[None],
        grad_in.astype(jnp.bfloat16)[None],
        grad_input_w,
        grad_output_w,
        grad_kernel,
        grad_mix,
        grad_first,
        grad_second,
        grad_group,
        grad_gate,
        grad_up,
        grad_down,
    )


def solution(mesh):
    in_specs = (
        P("rep", "seq", None),
        P("rep", None),
        P("rep", None),
        P("seq", None),
        P("seq", None),
        P(),
        P(),
        P(),
        P(),
        P(),
        P(None, "seq"),
        P(None, "seq"),
        P("seq", None),
        P("rep", "seq", None),
    )
    out_specs = (
        P("rep", "seq", None),
        P("rep", "seq", None),
        P("seq", None),
        P("seq", None),
        P(),
        P(),
        P(),
        P(),
        P(),
        P(None, "seq"),
        P(None, "seq"),
        P("seq", None),
    )
    return jax.shard_map(
        on_device, mesh=mesh, in_specs=in_specs, out_specs=out_specs, check_vma=False
    )
```

profile of v0, /device:TPU:0, one launch (start us, length us, event | category | flops | bytes accessed | tf_op | source)
XLA Modules:
  0.0 4016.5 jit_solution(8021908718773649853)
XLA Ops:
  9.3 132.8 %all-gather.5.cloned.1.call-done = bf16[1536,4608]{1,0:T(8,128)(2,1)} async-done(((bf16[192,4608]{1,0:T(8,128)(2,1)}), bf16[1536,4608]{1,0:T(8,128)(2,1)}) %all-gather.5.cloned.1.call-update) | async-done | bytes 14155792 | tf_op jit(solution)/shard_map/all_gather | solution.py:209
  178.6 39.8 collective-permute-done.1
  218.4 47.0 %collective-permute-done = bf16[256,3072]{1,0:T(8,128)(2,1)} collective-permute-done((bf16[256,3072]{1,0:T(8,128)(2,1)}, bf16[256,3072]{1,0:T(8,128)(2,1)}, u32[]{:S(2)}, u32[]{:S(2)}) %collective-permute-start) | collective-permute-done | bytes 1572896 | tf_op jit(solution)/shard_map/ppermute | solution.py:14
  286.9 341.3 %while.34 = (s32[]{:T(128)}, f32[8,256,2,96]{1,3,2,0:T(8,128)S(1)}, f32[8,2,256,1]{2,1,3,0:T(2,128)}, bf16[8,1024,2,96]{1,3,2,0:T(8,128)(2,1)}, f32[8,2,2]{2,1,0...) while((s32[]{:T(128)}, f32[8,256,2,96]{1,3,2,0:T(8,128)S(1)}, ...), condition=%wide.region_4.5_spmd.clone, body=%wide.region_1.4_spmd.clone.sunk | while | flops 281692032 | bytes 160720624 | solution.py:238
  652.1 102.0 %all-gather.9.cloned.1.call-done = bf16[2048,1536]{1,0:T(8,128)(2,1)} async-done(((bf16[256,1536]{1,0:T(8,128)(2,1)}), bf16[2048,1536]{1,0:T(8,128)(2,1)}) %all-gather.9.cloned.1.call-update) | async-done | bytes 6291472 | tf_op jit(solution)/shard_map/all_gather | solution.py:255
  767.9 51.8 %all-gather.11.cloned.1.call-done = bf16[2048,1536]{1,0:T(8,128)(2,1)} async-done(((bf16[256,1536]{1,0:T(8,128)(2,1)}), bf16[2048,1536]{1,0:T(8,128)(2,1)}) %all-gather.11.cloned.1.call-update) | async-done | bytes 6291472 | tf_op jit(solution)/shard_map/all_gather | solution.py:266
  848.9 61.1 %reduce-scatter.7.cloned.1.call-done = bf16[256,1536]{1,0:T(8,128)(2,1)} async-done(((bf16[2048,1536]{1,0:T(8,128)(2,1)}), bf16[256,1536]{1,0:T(8,128)(2,1)}) %reduce-scatter.7.cloned.1.call-update) | async-done | bytes 786448 | tf_op jit(solution)/shard_map/reduce_scatter | solution.py:280
  912.2 68.2 %reduce-scatter.5.cloned.1.call-done = bf16[256,1536]{1,0:T(8,128)(2,1)} async-done(((bf16[2048,1536]{1,0:T(8,128)(2,1)}), bf16[256,1536]{1,0:T(8,128)(2,1)}) %reduce-scatter.5.cloned.1.call-update) | async-done | bytes 786448 | tf_op jit(solution)/shard_map/reduce_scatter | solution.py:259
  1008.2 2550.7 %while.35 = (s32[]{:T(128)}, f32[8,261,2,96]{3,1,2,0:T(8,128)}, f32[8,1034,2,96]{1,3,2,0:T(8,128)}, f32[8,1024,2,96]{1,3,2,0:T(8,128)}, f32[8,2,6,11]{3,1,0,2:T(...) while((s32[]{:T(128)}, f32[8,261,2,96]{3,1,2,0:T(8,128)}, ...), condition=%wide.region_83.84_spmd.clone, body=%wide.region_13.83_spmd.clone.sunk | while | flops 1772737280 | bytes 370601792 | solution.py:304
  1041.3 36.7 multiply_reduce_fusion.77
  1163.3 124.6 %multiply_multiply_fusion.4 = f32[2,261,1034]{2,1,0:T(8,128)S(1)} fusion(f32[2,256,1024]{2,1,0:T(8,128)} %get-tuple-element.1464, f32[261,1034]{1,0:T(8,128)} %fusion.360, f32[2]{0:T(128)} %get-tuple-element.1396, f32[2]{0:T(128)} %get-tuple-element.1397, f32[2]{0:T(128)} %get-tuple-element.1398, f32[2]{0:T(128)} %get-tuple-element.1399, ...), kind=kLoop, calls=%fused_computation.436.clone.1 | loop fusion | flops 71786448 | bytes 5336168 | tf_op jit(solution)/shard_map/while/body/eval_jaxpr/mul | solution.py:121
  1478.6 124.6 %multiply_multiply_fusion.4 = f32[2,261,1034]{2,1,0:T(8,128)S(1)} fusion(f32[2,256,1024]{2,1,0:T(8,128)} %get-tuple-element.1464, f32[261,1034]{1,0:T(8,128)} %fusion.360, f32[2]{0:T(128)} %get-tuple-element.1396, f32[2]{0:T(128)} %get-tuple-element.1397, f32[2]{0:T(128)} %get-tuple-element.1398, f32[2]{0:T(128)} %get-tuple-element.1399, ...), kind=kLoop, calls=%fused_computation.436.clone.1 | loop fusion | flops 71786448 | bytes 5336168 | tf_op jit(solution)/shard_map/while/body/eval_jaxpr/mul | solution.py:121
  1671.8 36.7 multiply_reduce_fusion.77
  1793.8 124.6 %multiply_multiply_fusion.4 = f32[2,261,1034]{2,1,0:T(8,128)S(1)} fusion(f32[2,256,1024]{2,1,0:T(8,128)} %get-tuple-element.1464, f32[261,1034]{1,0:T(8,128)} %fusion.360, f32[2]{0:T(128)} %get-tuple-element.1396, f32[2]{0:T(128)} %get-tuple-element.1397, f32[2]{0:T(128)} %get-tuple-element.1398, f32[2]{0:T(128)} %get-tuple-element.1399, ...), kind=kLoop, calls=%fused_computation.436.clone.1 | loop fusion | flops 71786448 | bytes 5336168 | tf_op jit(solution)/shard_map/while/body/eval_jaxpr/mul | solution.py:121
  2109.1 124.6 %multiply_multiply_fusion.4 = f32[2,261,1034]{2,1,0:T(8,128)S(1)} fusion(f32[2,256,1024]{2,1,0:T(8,128)} %get-tuple-element.1464, f32[261,1034]{1,0:T(8,128)} %fusion.360, f32[2]{0:T(128)} %get-tuple-element.1396, f32[2]{0:T(128)} %get-tuple-element.1397, f32[2]{0:T(128)} %get-tuple-element.1398, f32[2]{0:T(128)} %get-tuple-element.1399, ...), kind=kLoop, calls=%fused_computation.436.clone.1 | loop fusion | flops 71786448 | bytes 5336168 | tf_op jit(solution)/shard_map/while/body/eval_jaxpr/mul | solution.py:121
  2424.4 124.6 %multiply_multiply_fusion.4 = f32[2,261,1034]{2,1,0:T(8,128)S(1)} fusion(f32[2,256,1024]{2,1,0:T(8,128)} %get-tuple-element.1464, f32[261,1034]{1,0:T(8,128)} %fusion.360, f32[2]{0:T(128)} %get-tuple-element.1396, f32[2]{0:T(128)} %get-tuple-element.1397, f32[2]{0:T(128)} %get-tuple-element.1398, f32[2]{0:T(128)} %get-tuple-element.1399, ...), kind=kLoop, calls=%fused_computation.436.clone.1 | loop fusion | flops 71786448 | bytes 5336168 | tf_op jit(solution)/shard_map/while/body/eval_jaxpr/mul | solution.py:121
  2617.6 36.7 multiply_reduce_fusion.77
  2739.6 124.6 %multiply_multiply_fusion.4 = f32[2,261,1034]{2,1,0:T(8,128)S(1)} fusion(f32[2,256,1024]{2,1,0:T(8,128)} %get-tuple-element.1464, f32[261,1034]{1,0:T(8,128)} %fusion.360, f32[2]{0:T(128)} %get-tuple-element.1396, f32[2]{0:T(128)} %get-tuple-element.1397, f32[2]{0:T(128)} %get-tuple-element.1398, f32[2]{0:T(128)} %get-tuple-element.1399, ...), kind=kLoop, calls=%fused_computation.436.clone.1 | loop fusion | flops 71786448 | bytes 5336168 | tf_op jit(solution)/shard_map/while/body/eval_jaxpr/mul | solution.py:121
  3054.9 124.6 %multiply_multiply_fusion.4 = f32[2,261,1034]{2,1,0:T(8,128)S(1)} fusion(f32[2,256,1024]{2,1,0:T(8,128)} %get-tuple-element.1464, f32[261,1034]{1,0:T(8,128)} %fusion.360, f32[2]{0:T(128)} %get-tuple-element.1396, f32[2]{0:T(128)} %get-tuple-element.1397, f32[2]{0:T(128)} %get-tuple-element.1398, f32[2]{0:T(128)} %get-tuple-element.1399, ...), kind=kLoop, calls=%fused_computation.436.clone.1 | loop fusion | flops 71786448 | bytes 5336168 | tf_op jit(solution)/shard_map/while/body/eval_jaxpr/mul | solution.py:121
  3370.2 124.6 %multiply_multiply_fusion.4 = f32[2,261,1034]{2,1,0:T(8,128)S(1)} fusion(f32[2,256,1024]{2,1,0:T(8,128)} %get-tuple-element.1464, f32[261,1034]{1,0:T(8,128)} %fusion.360, f32[2]{0:T(128)} %get-tuple-element.1396, f32[2]{0:T(128)} %get-tuple-element.1397, f32[2]{0:T(128)} %get-tuple-element.1398, f32[2]{0:T(128)} %get-tuple-element.1399, ...), kind=kLoop, calls=%fused_computation.436.clone.1 | loop fusion | flops 71786448 | bytes 5336168 | tf_op jit(solution)/shard_map/while/body/eval_jaxpr/mul | solution.py:121
  3620.5 38.8 collective-permute-done.6
  3693.2 147.7 %reduce-scatter.9.cloned.1.call-done = bf16[192,4608]{1,0:T(8,128)(2,1)} async-done(((bf16[1536,4608]{1,0:T(8,128)(2,1)}), bf16[192,4608]{1,0:T(8,128)(2,1)}) %reduce-scatter.9.cloned.1.call-update) | async-done | bytes 1769488 | tf_op jit(solution)/shard_map/reduce_scatter | solution.py:339
  3853.7 40.1 all-reduce.2
  3898.0 100.9 %all-reduce.6.cloned.1.call-done = (bf16[192,4608]{1,0:T(8,128)(2,1)}, bf16[192,1536]{1,0:T(8,128)(2,1)}, bf16[1536,512]{1,0:T(8,128)(2,1)}, bf16[1536,512]{1,0:T(8,128)(2,1)}, bf16[512,1536]{1,0:T(8,128)(2,1)}) async-done(((bf16[192,4608]{1,0:T(8,128)(2,1)}, bf16[192,1536]{1,0:T(8,128)(2,1)}, bf16[1536,512]{1,0:T(8,128)(2,1)}, bf16[1536,512]{1,0:T(8,128)(2,1)}, bf16[512,1536]{1,0:T(8,128)(2,1)}), ...) | async-done | bytes 7077904 | tf_op jit(solution)/shard_map/psum | solution.py:351
  (1999 shorter events, 2029.6 us)
Async XLA Ops:
  7.2 812.5 %copy-start = (bf16[512,1536]{1,0:T(8,128)(2,1)S(1)}, bf16[512,1536]{1,0:T(8,128)(2,1)}, u32[]{:S(2)}) copy-start(bf16[512,1536]{1,0:T(8,128)(2,1)} %param.30) | copy-start | bytes 4718596
  7.2 134.9 %copy-start.64 = (f32[1536]{0:T(1024)S(1)}, f32[1536]{0:T(1024)}, u32[]{:S(2)}) copy-start(f32[1536]{0:T(1024)} %param.25) | copy-start | bytes 18436
  7.2 134.8 %all-gather.5.cloned.1.call-start = ((), (), s32[]{:S(2)}) async-start(), calls=%async_computation.4 | async-start | bytes 15925248 | tf_op jit(solution)/shard_map/all_gather | solution.py:209
  8.0 634.8 %all-gather.7.cloned.1.call-start = ((), (), s32[]{:S(2)}) async-start(), calls=%async_computation.5 | async-start | bytes 5308416 | tf_op jit(solution)/shard_map/all_gather | solution.py:210
  9.3 142.0 %copy-start.72 = (f32[256]{0:T(256)}, f32[256]{0:T(256)S(1)}, u32[]{:S(2)}) copy-start(f32[256]{0:T(256)S(1)} %get-tuple-element.869) | copy-start | bytes 3076
  154.1 24.5 collective-permute-start.2
  157.4 61.1 %collective-permute-start.1 = (bf16[256,3072]{1,0:T(8,128)(2,1)}, bf16[256,3072]{1,0:T(8,128)(2,1)}, u32[]{:S(2)}, u32[]{:S(2)}) collective-permute-start(bf16[256,3072]{1,0:T(8,128)(2,1)} %slice.2477), channel_id=1, source_target_pairs={{0,2},{1,3},{2,4},{3,5},{4,6},{5,7},{8,10},{9,11},{10,12},{11,13},... | collective-permute-start | bytes 4718600 | tf_op jit(solution)/shard_map/ppermute | solution.py:14
  159.8 105.6 %collective-permute-start = (bf16[256,3072]{1,0:T(8,128)(2,1)}, bf16[256,3072]{1,0:T(8,128)(2,1)}, u32[]{:S(2)}, u32[]{:S(2)}) collective-permute-start(bf16[256,3072]{1,0:T(8,128)(2,1)} %slice.2477), channel_id=1, source_target_pairs={{0,3},{1,4},{2,5},{3,6},{4,7},{8,11},{9,12},{10,13},{11,14},{12,15... | collective-permute-start | bytes 4718600 | tf_op jit(solution)/shard_map/ppermute | solution.py:14
  162.3 591.8 %all-gather.9.cloned.1.call-start = ((), (), s32[]{:S(2)}) async-start(), calls=%async_computation.6 | async-start | bytes 7077888 | tf_op jit(solution)/shard_map/all_gather | solution.py:255
  165.4 3.6 collective-permute-start.3
  649.5 170.1 %all-gather.11.cloned.1.call-start = ((), (), s32[]{:S(2)}) async-start(), calls=%async_computation.8 | async-start | bytes 7077888 | tf_op jit(solution)/shard_map/all_gather | solution.py:266
  651.8 258.2 %reduce-scatter.7.cloned.1.call-start = ((), (), s32[]{:S(2)}) async-start(), calls=%async_computation.9 | async-start | bytes 7077888 | tf_op jit(solution)/shard_map/reduce_scatter | solution.py:280
  841.4 139.0 %reduce-scatter.5.cloned.1.call-start = ((), (), s32[]{:S(2)}) async-start(), calls=%async_computation.7 | async-start | bytes 7077888 | tf_op jit(solution)/shard_map/reduce_scatter | solution.py:259
  848.4 2844.7 %reduce-scatter.11.cloned.1.call-start = ((), (), s32[]{:S(2)}) async-start(), calls=%async_computation.11 | async-start | bytes 5308416 | tf_op jit(solution)/shard_map/reduce_scatter | solution.py:342
  1008.2 2832.7 %reduce-scatter.9.cloned.1.call-start = ((), (), s32[]{:S(2)}) async-start(), calls=%async_computation.10 | async-start | bytes 15925248 | tf_op jit(solution)/shard_map/reduce_scatter | solution.py:339
  3579.2 12.6 collective-permute-start.5
  3580.5 40.1 collective-permute-start.7
  3581.8 77.6 %collective-permute-start.6 = (bf16[256,3072]{0,1:T(8,128)(2,1)}, bf16[256,3072]{0,1:T(8,128)(2,1)}, u32[]{:S(2)}, u32[]{:S(2)}) collective-permute-start(bf16[256,3072]{0,1:T(8,128)(2,1)} %get-tuple-element.859), channel_id=1, source_target_pairs={{2,0},{3,1},{4,2},{5,3},{6,4},{7,5},{10,8},{11,9},{12,10},{13,11},... | collective-permute-start | bytes 4718600 | tf_op jit(solution)/shard_map/ppermute | solution.py:14
  3587.7 3.8 collective-permute-start.4
  3591.7 71.6 %copy-start.15 = (bf16[1,256,1536]{2,1,0:T(8,128)(2,1)S(1)}, bf16[1,256,1536]{2,1,0:T(8,128)(2,1)}, u32[]{:S(2)}) copy-start(bf16[1,256,1536]{2,1,0:T(8,128)(2,1)} %param.18) | copy-start | bytes 2359300
  3591.8 71.5 %copy-start.20 = (bf16[251,8,2,96]{0,3,2,1:T(8,128)(2,1)S(1)}, bf16[251,8,2,96]{0,3,2,1:T(8,128)(2,1)}, u32[]{:S(2)}) copy-start(bf16[251,8,2,96]{0,3,2,1:T(8,128)(2,1)} %slice.3701) | copy-start | bytes 2313220
  3591.8 71.5 %copy-start.65 = (f32[1536]{0:T(1024)S(1)}, f32[1536]{0:T(1024)}, u32[]{:S(2)}) copy-start(f32[1536]{0:T(1024)} %param.25) | copy-start | bytes 18436
  3591.8 71.5 %copy-start.73 = (f32[256]{0:T(256)S(1)}, f32[256]{0:T(256)}, u32[]{:S(2)}) copy-start(f32[256]{0:T(256)} %copy-done.72) | copy-start | bytes 3076
  3672.5 326.4 %all-reduce.6.cloned.1.call-start = ((), (), s32[]{:S(2)}) async-start(), calls=%async_computation.12 | async-start | bytes 14155776 | tf_op jit(solution)/shard_map/psum | solution.py:351
  (417 other events, 4098.7 us)
Sparse Core Ops, SparseCore 0:
  9.7 132.3 all-gather.4
  162.4 82.5 all-gather.6
  649.7 104.4 all-gather.8
  756.2 63.4 all-gather.10
  841.5 68.4 reduce-scatter.6
  912.1 68.1 reduce-scatter.4
  1008.3 53.3 reduce-scatter.10
  3672.7 168.1 reduce-scatter.8
  3846.3 152.5 all-reduce.5
where the time goes:
time: 4040 us; the launch traced here: 4020 us
  other arithmetic  2010 us (50%)
  local copies, waits for them, and re-layouts  853 us (21%)
  waiting for transfers between devices  821 us (20%)
  matrix products  225 us (6%)
    mul x8, other arithmetic, attend_group_back(): dlogits = convolve_back(dconv, kernel_g) * mask_ext * score_scale  997 us
    another operation x576, local copies, waits for them, and re-layouts, kernel_grads(): entries.append(jnp.stack(line_sums, axis=-1))  678 us
    reduce_sum x32, other arithmetic, kernel_grads(): line_sums.append(jnp.sum(grads * window_part, axis=(1, 2)))  334 us
    reduce_sum x8, other arithmetic, attend_group_back(): dconv = prob * (dprob - jnp.sum(prob * dprob, axis=-1, keepdims=True))  294 us
    reduce_max x8, other arithmetic, attend_group(): peak = jnp.max(jnp.where(allowed, conv, -1e+30), axis=-1, keepdims=True)  277 us
    ppermute x8, waiting for transfers between devices, from_behind(): return lax.ppermute(x, axis, pairs)  155 us
    reduce_scatter x1, waiting for transfers between devices, on_device(): lax.psum_scatter(whole_input_grad.astype(jnp.bfloat16), 'seq', scatter_di...  148 us
    all_gather x1, waiting for transfers between devices, on_device(): lax.all_gather(input_weight, 'seq', axis=0, tiled=True)  133 us
  transfers between devices with their start and end apart: 17, of which 12 were waited for; matrix products, arithmetic and copies ran while one was open for 74% of the time, Pallas kernels for 0%

commit v1 on v0

--- a/solution.py
+++ b/solution.py
@@ -348,7 +348,9 @@
         (kernel_part, dmixing, first_part, second_part, group_part), ("rep", "seq")
     )
     grad_input_w, grad_output_w, grad_gate, grad_up, grad_down = (
-        lax.psum(input_shard.astype(jnp.bfloat16), "rep").astype(jnp.float32),
+        lax.all_gather(input_shard.astype(jnp.bfloat16), axis_name="rep")
+        .sum(axis=0)
+        .astype(jnp.float32),
         lax.psum(output_shard.astype(jnp.bfloat16), "rep").astype(jnp.float32),
         lax.psum(grad_gate.astype(jnp.bfloat16), "rep").astype(jnp.float32),
         lax.psum(grad_up.astype(jnp.bfloat16), "rep").astype(jnp.float32),

time: 4040 us -> 3010 us (0.75)
  other arithmetic: 2010 us -> 1380 us
  local copies, waits for them, and re-layouts: 853 us -> 427 us
  waiting for transfers between devices: 821 us -> 862 us
    mul x8, other arithmetic: 997 us -> 367 us  [attend_group_back(): dlogits = convolve_back(dconv, kernel_g) * mask_ext * score_scale]
    another operation x576, local copies, waits for them, and re-layouts: 678 us -> 235 us  [kernel_grads(): entries.append(jnp.stack(line_sums, axis=-1))]
    all_gather x0 -> x1, waiting for transfers between devices: none -> 69.5 us  [on_device(): lax.all_gather(input_shard.astype(jnp.bfloat16), axis_name='rep')]
  transfers between devices with their start and end apart: 17 -> 18, of which waited for: 12 -> 13; matrix products, arithmetic and copies ran while one was open for 74% -> 66% of each run, Pallas kernels for 0% -> 0%
where the time goes in v1:
time: 3010 us; the launch traced here: 3000 us
  other arithmetic  1380 us (46%)
  waiting for transfers between devices  862 us (29%)
  local copies, waits for them, and re-layouts  427 us (14%)
  matrix products  243 us (8%)
  blocking collectives  40.2 us (1%)
    mul x8, other arithmetic, attend_group_back(): dlogits = convolve_back(dconv, kernel_g) * mask_ext * score_scale  367 us
    reduce_sum x32, other arithmetic, kernel_grads(): line_sums.append(jnp.sum(grads * window_part, axis=(1, 2)))  335 us
    reduce_sum x8, other arithmetic, attend_group_back(): dconv = prob * (dprob - jnp.sum(prob * dprob, axis=-1, keepdims=True))  294 us
    reduce_max x8, other arithmetic, attend_group(): peak = jnp.max(jnp.where(allowed, conv, -1e+30), axis=-1, keepdims=True)  277 us
    another operation x576, local copies, waits for them, and re-layouts, kernel_grads(): entries.append(jnp.stack(line_sums, axis=-1))  235 us
    reduce_scatter x1, waiting for transfers between devices, on_device(): lax.psum_scatter(whole_input_grad.astype(jnp.bfloat16), 'seq', scatter_di...  156 us
    ppermute x8, waiting for transfers between devices, from_behind(): return lax.ppermute(x, axis, pairs)  147 us
    all_gather x1, waiting for transfers between devices, on_device(): lax.all_gather(input_weight, 'seq', axis=0, tiled=True)  133 us
  transfers between devices with their start and end apart: 18, of which 13 were waited for; matrix products, arithmetic and copies ran while one was open for 66% of the time, Pallas kernels for 0%

profile of v1, /device:TPU:0, one launch (start us, length us, event | category | flops | bytes accessed | tf_op | source)
XLA Modules:
  0.0 2997.7 jit_solution(7229267215168401925)
XLA Ops:
  9.3 132.8 %all-gather.7.cloned.1.call-done = bf16[1536,4608]{1,0:T(8,128)(2,1)} async-done(((bf16[192,4608]{1,0:T(8,128)(2,1)}), bf16[1536,4608]{1,0:T(8,128)(2,1)}) %all-gather.7.cloned.1.call-update) | async-done | bytes 14155792 | tf_op jit(solution)/shard_map/all_gather | solution.py:209
  209.0 52.4 %collective-permute-done.1 = bf16[256,3072]{1,0:T(8,128)(2,1)} collective-permute-done((bf16[256,3072]{1,0:T(8,128)(2,1)}, bf16[256,3072]{1,0:T(8,128)(2,1)}, u32[]{:S(2)}, u32[]{:S(2)}) %collective-permute-start.1) | collective-permute-done | bytes 1572896 | tf_op jit(solution)/shard_map/ppermute | solution.py:14
  282.9 336.9 %while.34 = (s32[]{:T(128)}, f32[8,256,2,96]{1,3,2,0:T(8,128)}, f32[8,2,256,1]{2,1,3,0:T(2,128)}, bf16[8,1024,2,96]{1,3,2,0:T(8,128)(2,1)}, f32[8,2,2]{2,1,0:T(2...) while((s32[]{:T(128)}, f32[8,256,2,96]{1,3,2,0:T(8,128)}, ...), condition=%wide.region_4.5_spmd.clone, body=%wide.region_1.4_spmd.clone.sunk | while | flops 281692032 | bytes 160720112 | solution.py:238
  647.1 103.4 %all-gather.11.cloned.1.call-done = bf16[2048,1536]{1,0:T(8,128)(2,1)} async-done(((bf16[256,1536]{1,0:T(8,128)(2,1)}), bf16[2048,1536]{1,0:T(8,128)(2,1)}) %all-gather.11.cloned.1.call-update) | async-done | bytes 6291472 | tf_op jit(solution)/shard_map/all_gather | solution.py:255
  764.2 51.8 %all-gather.13.cloned.1.call-done = bf16[2048,1536]{1,0:T(8,128)(2,1)} async-done(((bf16[256,1536]{1,0:T(8,128)(2,1)}), bf16[2048,1536]{1,0:T(8,128)(2,1)}) %all-gather.13.cloned.1.call-update) | async-done | bytes 6291472 | tf_op jit(solution)/shard_map/all_gather | solution.py:266
  844.9 61.5 %reduce-scatter.7.cloned.1.call-done = bf16[256,1536]{1,0:T(8,128)(2,1)} async-done(((bf16[2048,1536]{1,0:T(8,128)(2,1)}), bf16[256,1536]{1,0:T(8,128)(2,1)}) %reduce-scatter.7.cloned.1.call-update) | async-done | bytes 786448 | tf_op jit(solution)/shard_map/reduce_scatter | solution.py:280
  908.6 68.2 %reduce-scatter.5.cloned.1.call-done = bf16[256,1536]{1,0:T(8,128)(2,1)} async-done(((bf16[2048,1536]{1,0:T(8,128)(2,1)}), bf16[256,1536]{1,0:T(8,128)(2,1)}) %reduce-scatter.5.cloned.1.call-update) | async-done | bytes 786448 | tf_op jit(solution)/shard_map/reduce_scatter | solution.py:259
  1006.8 1488.4 %while.35 = (s32[]{:T(128)}, f32[8,261,2,96]{3,1,2,0:T(8,128)}, f32[8,1034,2,96]{1,3,2,0:T(8,128)}, f32[8,1024,2,96]{1,3,2,0:T(8,128)}, f32[8,2,6,11]{3,1,0,2:T(...) while((s32[]{:T(128)}, f32[8,261,2,96]{3,1,2,0:T(8,128)}, ...), condition=%wide.region_83.84_spmd.clone, body=%wide.region_13.83_spmd.clone.sunk | while | flops 1772737280 | bytes 383704672 | solution.py:304
  1018.0 36.8 %multiply_reduce_fusion.77 = (f32[2,256]{1,0:T(2,128)S(1)}, f32[2,256,1024]{2,1,0:T(8,128)S(1)}) fusion(f32[256,1024]{1,0:T(8,128)} %get-tuple-element.1391, f32[2]{0:T(128)} %get-tuple-element.1392, f32[256,1024]{1,0:T(8,128)S(1)} %get-tuple-element.1393, f32[2]{0:T(128)} %get-tuple-element.1394, f32[2,256]{1,0:T(2,128)S(1)} %fusion.359, ...), kind=kLoop, calls=%fused_computation.507.clone.1 | loop fusion | flops 72351232 | bytes 142873120 | tf_op jit(solution)/shard_map/while/body/eval_jaxpr/reduce_sum | solution.py:119
  1138.9 45.9 %multiply_multiply_fusion.4 = f32[2,261,1034]{2,1,0:T(8,128)} fusion(f32[2,256,1024]{2,1,0:T(8,128)S(1)} %copy-done.2, f32[261,1034]{1,0:T(8,128)S(1)} %fusion.360, f32[2]{0:T(128)S(1)} %get-tuple-element.1395, f32[2]{0:T(128)S(1)} %get-tuple-element.1396, f32[2]{0:T(128)S(1)} %get-tuple-element.1397, f32[2]{0:T(128)S(1)} %get-tuple-element.1398, ...), kind=kLoop, calls=%fused_computation.436.clone.1 | loop fusion | flops 71786448 | bytes 5336168 | tf_op jit(solution)/shard_map/while/body/eval_jaxpr/mul | solution.py:121
  1203.0 36.8 %multiply_reduce_fusion.77 = (f32[2,256]{1,0:T(2,128)S(1)}, f32[2,256,1024]{2,1,0:T(8,128)S(1)}) fusion(f32[256,1024]{1,0:T(8,128)} %get-tuple-element.1391, f32[2]{0:T(128)} %get-tuple-element.1392, f32[256,1024]{1,0:T(8,128)S(1)} %get-tuple-element.1393, f32[2]{0:T(128)} %get-tuple-element.1394, f32[2,256]{1,0:T(2,128)S(1)} %fusion.359, ...), kind=kLoop, calls=%fused_computation.507.clone.1 | loop fusion | flops 72351232 | bytes 142873120 | tf_op jit(solution)/shard_map/while/body/eval_jaxpr/reduce_sum | solution.py:119
  1323.9 45.9 %multiply_multiply_fusion.4 = f32[2,261,1034]{2,1,0:T(8,128)} fusion(f32[2,256,1024]{2,1,0:T(8,128)S(1)} %copy-done.2, f32[261,1034]{1,0:T(8,128)S(1)} %fusion.360, f32[2]{0:T(128)S(1)} %get-tuple-element.1395, f32[2]{0:T(128)S(1)} %get-tuple-element.1396, f32[2]{0:T(128)S(1)} %get-tuple-element.1397, f32[2]{0:T(128)S(1)} %get-tuple-element.1398, ...), kind=kLoop, calls=%fused_computation.436.clone.1 | loop fusion | flops 71786448 | bytes 5336168 | tf_op jit(solution)/shard_map/while/body/eval_jaxpr/mul | solution.py:121
  1508.9 45.9 %multiply_multiply_fusion.4 = f32[2,261,1034]{2,1,0:T(8,128)} fusion(f32[2,256,1024]{2,1,0:T(8,128)S(1)} %copy-done.2, f32[261,1034]{1,0:T(8,128)S(1)} %fusion.360, f32[2]{0:T(128)S(1)} %get-tuple-element.1395, f32[2]{0:T(128)S(1)} %get-tuple-element.1396, f32[2]{0:T(128)S(1)} %get-tuple-element.1397, f32[2]{0:T(128)S(1)} %get-tuple-element.1398, ...), kind=kLoop, calls=%fused_computation.436.clone.1 | loop fusion | flops 71786448 | bytes 5336168 | tf_op jit(solution)/shard_map/while/body/eval_jaxpr/mul | solution.py:121
  1573.0 36.8 %multiply_reduce_fusion.77 = (f32[2,256]{1,0:T(2,128)S(1)}, f32[2,256,1024]{2,1,0:T(8,128)S(1)}) fusion(f32[256,1024]{1,0:T(8,128)} %get-tuple-element.1391, f32[2]{0:T(128)} %get-tuple-element.1392, f32[256,1024]{1,0:T(8,128)S(1)} %get-tuple-element.1393, f32[2]{0:T(128)} %get-tuple-element.1394, f32[2,256]{1,0:T(2,128)S(1)} %fusion.359, ...), kind=kLoop, calls=%fused_computation.507.clone.1 | loop fusion | flops 72351232 | bytes 142873120 | tf_op jit(solution)/shard_map/while/body/eval_jaxpr/reduce_sum | solution.py:119
  1694.0 45.9 %multiply_multiply_fusion.4 = f32[2,261,1034]{2,1,0:T(8,128)} fusion(f32[2,256,1024]{2,1,0:T(8,128)S(1)} %copy-done.2, f32[261,1034]{1,0:T(8,128)S(1)} %fusion.360, f32[2]{0:T(128)S(1)} %get-tuple-element.1395, f32[2]{0:T(128)S(1)} %get-tuple-element.1396, f32[2]{0:T(128)S(1)} %get-tuple-element.1397, f32[2]{0:T(128)S(1)} %get-tuple-element.1398, ...), kind=kLoop, calls=%fused_computation.436.clone.1 | loop fusion | flops 71786448 | bytes 5336168 | tf_op jit(solution)/shard_map/while/body/eval_jaxpr/mul | solution.py:121
  1879.0 45.9 %multiply_multiply_fusion.4 = f32[2,261,1034]{2,1,0:T(8,128)} fusion(f32[2,256,1024]{2,1,0:T(8,128)S(1)} %copy-done.2, f32[261,1034]{1,0:T(8,128)S(1)} %fusion.360, f32[2]{0:T(128)S(1)} %get-tuple-element.1395, f32[2]{0:T(128)S(1)} %get-tuple-element.1396, f32[2]{0:T(128)S(1)} %get-tuple-element.1397, f32[2]{0:T(128)S(1)} %get-tuple-element.1398, ...), kind=kLoop, calls=%fused_computation.436.clone.1 | loop fusion | flops 71786448 | bytes 5336168 | tf_op jit(solution)/shard_map/while/body/eval_jaxpr/mul | solution.py:121
  2064.0 45.9 %multiply_multiply_fusion.4 = f32[2,261,1034]{2,1,0:T(8,128)} fusion(f32[2,256,1024]{2,1,0:T(8,128)S(1)} %copy-done.2, f32[261,1034]{1,0:T(8,128)S(1)} %fusion.360, f32[2]{0:T(128)S(1)} %get-tuple-element.1395, f32[2]{0:T(128)S(1)} %get-tuple-element.1396, f32[2]{0:T(128)S(1)} %get-tuple-element.1397, f32[2]{0:T(128)S(1)} %get-tuple-element.1398, ...), kind=kLoop, calls=%fused_computation.436.clone.1 | loop fusion | flops 71786448 | bytes 5336168 | tf_op jit(solution)/shard_map/while/body/eval_jaxpr/mul | solution.py:121
  2249.0 45.9 %multiply_multiply_fusion.4 = f32[2,261,1034]{2,1,0:T(8,128)} fusion(f32[2,256,1024]{2,1,0:T(8,128)S(1)} %copy-done.2, f32[261,1034]{1,0:T(8,128)S(1)} %fusion.360, f32[2]{0:T(128)S(1)} %get-tuple-element.1395, f32[2]{0:T(128)S(1)} %get-tuple-element.1396, f32[2]{0:T(128)S(1)} %get-tuple-element.1397, f32[2]{0:T(128)S(1)} %get-tuple-element.1398, ...), kind=kLoop, calls=%fused_computation.436.clone.1 | loop fusion | flops 71786448 | bytes 5336168 | tf_op jit(solution)/shard_map/while/body/eval_jaxpr/mul | solution.py:121
  2434.0 45.9 %multiply_multiply_fusion.4 = f32[2,261,1034]{2,1,0:T(8,128)} fusion(f32[2,256,1024]{2,1,0:T(8,128)S(1)} %copy-done.2, f32[261,1034]{1,0:T(8,128)S(1)} %fusion.360, f32[2]{0:T(128)S(1)} %get-tuple-element.1395, f32[2]{0:T(128)S(1)} %get-tuple-element.1396, f32[2]{0:T(128)S(1)} %get-tuple-element.1397, f32[2]{0:T(128)S(1)} %get-tuple-element.1398, ...), kind=kLoop, calls=%fused_computation.436.clone.1 | loop fusion | flops 71786448 | bytes 5336168 | tf_op jit(solution)/shard_map/while/body/eval_jaxpr/mul | solution.py:121
  2528.1 54.1 %collective-permute-done.6 = bf16[256,3072]{0,1:T(8,128)(2,1)} collective-permute-done((bf16[256,3072]{0,1:T(8,128)(2,1)}, bf16[256,3072]{0,1:T(8,128)(2,1)}, u32[]{:S(2)}, u32[]{:S(2)}) %collective-permute-start.6) | collective-permute-done | bytes 1572896 | tf_op jit(solution)/shard_map/ppermute | solution.py:14
  2621.2 156.1 %reduce-scatter.9.cloned.1.call-done = bf16[192,4608]{1,0:T(8,128)(2,1)} async-done(((bf16[1536,4608]{1,0:T(8,128)(2,1)}), bf16[192,4608]{1,0:T(8,128)(2,1)}) %reduce-scatter.9.cloned.1.call-update) | async-done | bytes 1769488 | tf_op jit(solution)/shard_map/reduce_scatter | solution.py:339
  2789.5 40.2 %all-reduce.2 = (f32[16,6,11]{2,0,1:T(8,128)S(1)}, f32[8,2,2]{0,2,1:T(2,128)}, f32[1536]{0:T(1024)}, f32[1536]{0:T(1024)}, f32[1536]{0:T(1024)}) all-reduce(f32[16,6,11]{2,0,1:T(8,128)} %bitcast.784, f32[8,2,2]{0,2,1:T(2,128)} %copy.255, f32[1536]{0:T(1024)} %get-tuple-element.619, ...), channel_id=1, replica_groups=mesh['rep'=4,'seq'=8] {'rep','seq'}, use_global_device_ids=true, to_apply=%region_89.90 | all-reduce | flops 5696 | bytes 45568 | tf_op jit(solution)/shard_map/psum | solution.py:347
  2833.9 70.9 %all-reduce.6.cloned.1.call-done = (bf16[192,1536]{1,0:T(8,128)(2,1)}, bf16[1536,512]{1,0:T(8,128)(2,1)}, bf16[1536,512]{1,0:T(8,128)(2,1)}, bf16[512,1536]{1,0:T(8,128)(2,1)}) async-done(((bf16[192,1536]{1,0:T(8,128)(2,1)}, bf16[1536,512]{1,0:T(8,128)(2,1)}, bf16[1536,512]{1,0:T(8,128)(2,1)}, bf16[512,1536]{1,0:T(8,128)(2,1)}), (bf16[192,1536]{1,0:T(8,128)(2,1)}, bf16[1536,512]{1,0:T(8,128)(2,1)}, ...) | async-done | bytes 5308432 | tf_op jit(solution)/shard_map/psum | solution.py:354
  2913.8 69.5 %all-gather.15.cloned.1.call-done = bf16[768,4608]{1,0:T(8,128)(2,1)} async-done(((bf16[192,4608]{1,0:T(8,128)(2,1)}), bf16[768,4608]{1,0:T(8,128)(2,1)}) %all-gather.15.cloned.1.call-update) | async-done | bytes 7077904 | tf_op jit(solution)/shard_map/all_gather | solution.py:351
  (2133 shorter events, 1628.3 us)
Async XLA Ops:
  7.2 808.9 %copy-start = (bf16[512,1536]{1,0:T(8,128)(2,1)S(1)}, bf16[512,1536]{1,0:T(8,128)(2,1)}, u32[]{:S(2)}) copy-start(bf16[512,1536]{1,0:T(8,128)(2,1)} %param.30) | copy-start | bytes 4718596
  7.2 134.9 %copy-start.69 = (f32[1536]{0:T(1024)S(1)}, f32[1536]{0:T(1024)}, u32[]{:S(2)}) copy-start(f32[1536]{0:T(1024)} %param.25) | copy-start | bytes 18436
  7.2 134.8 %all-gather.7.cloned.1.call-start = ((), (), s32[]{:S(2)}) async-start(), calls=%async_computation.4 | async-start | bytes 15925248 | tf_op jit(solution)/shard_map/all_gather | solution.py:209
  8.0 631.3 %all-gather.9.cloned.1.call-start = ((), (), s32[]{:S(2)}) async-start(), calls=%async_computation.5 | async-start | bytes 5308416 | tf_op jit(solution)/shard_map/all_gather | solution.py:210
  9.3 142.0 %copy-start.74 = (f32[256]{0:T(256)}, f32[256]{0:T(256)S(1)}, u32[]{:S(2)}) copy-start(f32[256]{0:T(256)S(1)} %get-tuple-element.868) | copy-start | bytes 3076
  154.1 55.0 %collective-permute-start = (bf16[256,3072]{1,0:T(8,128)(2,1)}, bf16[256,3072]{1,0:T(8,128)(2,1)}, u32[]{:S(2)}, u32[]{:S(2)}) collective-permute-start(bf16[256,3072]{1,0:T(8,128)(2,1)} %slice.2477), channel_id=1, source_target_pairs={{0,3},{1,4},{2,5},{3,6},{4,7},{8,11},{9,12},{10,13},{11,14},{12,15... | collective-permute-start | bytes 4718600 | tf_op jit(solution)/shard_map/ppermute | solution.py:14
  156.5 104.9 %collective-permute-start.1 = (bf16[256,3072]{1,0:T(8,128)(2,1)}, bf16[256,3072]{1,0:T(8,128)(2,1)}, u32[]{:S(2)}, u32[]{:S(2)}) collective-permute-start(bf16[256,3072]{1,0:T(8,128)(2,1)} %slice.2477), channel_id=1, source_target_pairs={{0,2},{1,3},{2,4},{3,5},{4,6},{5,7},{8,10},{9,11},{10,12},{11,13},... | collective-permute-start | bytes 4718600 | tf_op jit(solution)/shard_map/ppermute | solution.py:14
  161.3 100.1 %collective-permute-start.2 = (bf16[256,3072]{1,0:T(8,128)(2,1)}, bf16[256,3072]{1,0:T(8,128)(2,1)}, u32[]{:S(2)}, u32[]{:S(2)}) collective-permute-start(bf16[256,3072]{1,0:T(8,128)(2,1)} %slice.2477), channel_id=1, source_target_pairs={{0,1},{1,2},{2,3},{3,4},{4,5},{5,6},{6,7},{8,9},{9,10},{10,11},{11... | collective-permute-start | bytes 4718600 | tf_op jit(solution)/shard_map/ppermute | solution.py:14
  163.7 586.8 %all-gather.11.cloned.1.call-start = ((), (), s32[]{:S(2)}) async-start(), calls=%async_computation.6 | async-start | bytes 7077888 | tf_op jit(solution)/shard_map/all_gather | solution.py:255
  165.8 2.9 collective-permute-start.3
  645.9 170.1 %all-gather.13.cloned.1.call-start = ((), (), s32[]{:S(2)}) async-start(), calls=%async_computation.8 | async-start | bytes 7077888 | tf_op jit(solution)/shard_map/all_gather | solution.py:266
  647.0 259.3 %reduce-scatter.7.cloned.1.call-start = ((), (), s32[]{:S(2)}) async-start(), calls=%async_computation.9 | async-start | bytes 7077888 | tf_op jit(solution)/shard_map/reduce_scatter | solution.py:280
  837.8 139.0 %reduce-scatter.5.cloned.1.call-start = ((), (), s32[]{:S(2)}) async-start(), calls=%async_computation.7 | async-start | bytes 7077888 | tf_op jit(solution)/shard_map/reduce_scatter | solution.py:259
  844.8 1776.3 %reduce-scatter.11.cloned.1.call-start = ((), (), s32[]{:S(2)}) async-start(), calls=%async_computation.11 | async-start | bytes 5308416 | tf_op jit(solution)/shard_map/reduce_scatter | solution.py:342
  983.8 1793.5 %reduce-scatter.9.cloned.1.call-start = ((), (), s32[]{:S(2)}) async-start(), calls=%async_computation.10 | async-start | bytes 15925248 | tf_op jit(solution)/shard_map/reduce_scatter | solution.py:339
  2515.4 12.6 collective-permute-start.5
  2516.7 65.5 %collective-permute-start.6 = (bf16[256,3072]{0,1:T(8,128)(2,1)}, bf16[256,3072]{0,1:T(8,128)(2,1)}, u32[]{:S(2)}, u32[]{:S(2)}) collective-permute-start(bf16[256,3072]{0,1:T(8,128)(2,1)} %get-tuple-element.858), channel_id=1, source_target_pairs={{2,0},{3,1},{4,2},{5,3},{6,4},{7,5},{10,8},{11,9},{12,10},{13,11},... | collective-permute-start | bytes 4718600 | tf_op jit(solution)/shard_map/ppermute | solution.py:14
  2518.0 69.1 %collective-permute-start.7 = (bf16[256,3072]{0,1:T(8,128)(2,1)}, bf16[256,3072]{0,1:T(8,128)(2,1)}, u32[]{:S(2)}, u32[]{:S(2)}) collective-permute-start(bf16[256,3072]{0,1:T(8,128)(2,1)} %get-tuple-element.857), channel_id=1, source_target_pairs={{3,0},{4,1},{5,2},{6,3},{7,4},{11,8},{12,9},{13,10},{14,11},{15,12... | collective-permute-start | bytes 4718600 | tf_op jit(solution)/shard_map/ppermute | solution.py:14
  2524.0 3.8 collective-permute-start.4
  2528.0 63.1 %copy-start.18 = (bf16[1,256,1536]{2,1,0:T(8,128)(2,1)S(1)}, bf16[1,256,1536]{2,1,0:T(8,128)(2,1)}, u32[]{:S(2)}) copy-start(bf16[1,256,1536]{2,1,0:T(8,128)(2,1)} %param.18) | copy-start | bytes 2359300
  2528.0 63.1 %copy-start.24 = (bf16[251,8,2,96]{0,3,2,1:T(8,128)(2,1)S(1)}, bf16[251,8,2,96]{0,3,2,1:T(8,128)(2,1)}, u32[]{:S(2)}) copy-start(bf16[251,8,2,96]{0,3,2,1:T(8,128)(2,1)} %slice.3701) | copy-start | bytes 2313220
  2600.4 304.4 %all-reduce.6.cloned.1.call-start = ((), (), s32[]{:S(2)}) async-start(), calls=%async_computation.13 | async-start | bytes 10616832 | tf_op jit(solution)/shard_map/psum | solution.py:354
  2621.1 156.2 %copy-start.83 = (f32[8,2,2]{2,1,0:T(2,128)S(1)}, f32[8,2,2]{2,1,0:T(2,128)}, u32[]{:S(2)}) copy-start(f32[8,2,2]{2,1,0:T(2,128)} %get-tuple-element.270) | copy-start | bytes 388
  2621.1 362.1 %all-gather.15.cloned.1.call-start = ((), (), s32[]{:S(2)}) async-start(), calls=%async_computation.12 | async-start | bytes 8847360 | tf_op jit(solution)/shard_map/all_gather | solution.py:351
  (483 other events, 4302.4 us)
Sparse Core Ops, SparseCore 0:
  9.7 132.3 all-gather.6
  163.9 82.5 all-gather.8
  646.0 104.4 all-gather.10
  752.6 63.3 all-gather.12
  837.9 68.4 reduce-scatter.6
  908.5 68.1 reduce-scatter.4
  984.0 53.3 reduce-scatter.10
  2600.5 176.7 reduce-scatter.8
  2782.2 122.5 all-reduce.5
  2906.5 76.6 all-gather.14
